TPU v7x, 1024 devices: a whole 8x8x8 slice. The times are simulated.
1024 devices in a mesh: gx: 8 (over x), gy: 8 (over z), gz: 16 (over y, core).
Axes of the slice: x: 8, y: 8, z: 8, core: 2. Of those that a mesh axis runs over, the one named last changes fastest.
Arguments:
- offsets: float32 [3, 16, 16, 32, 128], P(None, 'gx', 'gy', 'gz'), may hold values from 0 to 1
- masses: float32 [16, 16, 32, 128], P('gx', 'gy', 'gz'), may hold values from 0.12 to 3
- smoothing: float32 [16, 16, 32, 128], P('gx', 'gy', 'gz'), may hold values from 0.6 to 0.75
- velocity: float32 [3, 16, 16, 32, 128], P(None, 'gx', 'gy', 'gz'), may hold values from -6 to 6
- energy: float32 [16, 16, 32, 128], P('gx', 'gy', 'gz'), may hold values from 0.3 to 3
- active: int32 [16, 16, 32, 128], P('gx', 'gy', 'gz'), may hold values from 0 to 1, as said below
Outputs:
- density: float32 [16, 16, 32, 128], P('gx', 'gy', 'gz')
- acceleration: float32 [3, 16, 16, 32, 128], P(None, 'gx', 'gy', 'gz')
- heating: float32 [16, 16, 32, 128], P('gx', 'gy', 'gz')
Inputs may be any that keep to these rules, and one draw needn't show every extreme that they name: The share of active particles differs from cell to cell, from none to all.
All inputs are finite; a program needn't handle non-finite values.
Results may differ from a plain program's by a relative error of at most 0.0003.
Values sent between devices are 32-bit elements; how exact they have to be, the bound alone decides.
A program may use at most 32 MiB of HBM per device.

v0:
```python
import functools

import jax
import jax.numpy as jnp
from jax import lax
from jax.experimental import pallas as pl
from jax.experimental.pallas import tpu as pltpu
from jax.sharding import PartitionSpec as P

MESH = pl.DeviceIdType.MESH
AXES = ("gx", "gy", "gz")
KERNEL_NORM = 2.5464790894703255
ETA = 2.3
GAMMA = 5.0 / 3.0
ROOT3 = 3.0**0.5
TINY = 1e-12
DIRECTIONS = [
    (dx, dy, dz) for dx in (-1, 0, 1) for dy in (-1, 0, 1) for dz in (-1, 0, 1) if (dx, dy, dz) != (0, 0, 0)
]
OFFSETS = [(a * 16 + b * 4 + c) for a in range(3) for b in range(3) for c in range(3)]


def source_part(step):
    return slice(2, 3) if step == 1 else slice(1, 2) if step == -1 else slice(1, 3)


def landing_part(step):
    return slice(0, 1) if step == 1 else slice(3, 4) if step == -1 else slice(1, 3)


def neighbour(direction):
    found = {}
    for axis, step in zip(AXES, direction):
        count = lax.axis_size(axis)
        found[axis] = lax.rem(lax.axis_index(axis) + count + step, count)
    return tuple(found[axis] for axis in AXES)


def exchange(buffer, send_sem, recv_sem):
    copies = []
    for place, direction in enumerate(DIRECTIONS):
        here = tuple(source_part(step) for step in direction)
        there = tuple(landing_part(step) for step in direction)
        copies.append(
            pltpu.make_async_remote_copy(
                src_ref=buffer.at[here],
                dst_ref=buffer.at[there],
                send_sem=send_sem.at[place],
                recv_sem=recv_sem.at[place],
                device_id=neighbour(direction),
                device_id_type=MESH,
            )
        )
    return copies


def rounded(value):
    return value.astype(jnp.bfloat16).astype(jnp.float32)


def thirds(value):
    high = rounded(value)
    rest = value - high
    middle = rounded(rest)
    return high, middle, rest - middle


def cube_root(value):
    guess = jnp.exp(jnp.log(value) * (1.0 / 3.0))
    return (2.0 * guess + value / (guess * guess)) * (1.0 / 3.0)


def fold(tile):
    parts = [tile[8 * i : 8 * i + 8] for i in range(tile.shape[0] // 8)]
    while len(parts) > 1:
        parts = [parts[i] + parts[i + 1] for i in range(0, len(parts) - 1, 2)] + (
            [parts[-1]] if len(parts) % 2 else []
        )
    return parts[0]


def placed(tile, cell_x, cell_y, cell_z):
    row = lax.broadcasted_iota(jnp.int32, (8, 128), 0)
    shift = jnp.where(
        row == 0,
        cell_x.astype(jnp.float32) - 2.0,
        jnp.where(row == 1, cell_y.astype(jnp.float32) - 2.0, jnp.where(row == 2, cell_z.astype(jnp.float32) - 2.0, 0.0)),
    )
    return row, tile + shift


def kernel(
    off_ref,
    mass_ref,
    smooth_ref,
    vel_ref,
    energy_ref,
    active_ref,
    dens_ref,
    acc_ref,
    heat_ref,
    field,
    late,
    feat,
    tfeat,
    mass_b,
    len_b,
    col_a,
    col_b,
    dist,
    square,
    send_sem,
    recv_sem,
    send_late,
    recv_late,
):
    f32 = jnp.float32
    barrier = pltpu.get_barrier_semaphore()
    for direction in DIRECTIONS:
        pl.semaphore_signal(barrier, inc=1, device_id=neighbour(direction), device_id_type=MESH)
    for x in range(2):
        for y in range(2):
            for z in range(2):
                for c in range(3):
                    field[1 + x, 1 + y, 1 + z, c : c + 1] = off_ref[c, x, y, z : z + 1]
                    field[1 + x, 1 + y, 1 + z, 4 + c : 5 + c] = vel_ref[c, x, y, z : z + 1]
                field[1 + x, 1 + y, 1 + z, 3:4] = mass_ref[x, y, z : z + 1]
                field[1 + x, 1 + y, 1 + z, 7:8] = energy_ref[x, y, z : z + 1]
    pl.semaphore_wait(barrier, len(DIRECTIONS))
    first = exchange(field, send_sem, recv_sem)
    for copy in first:
        copy.start()

    lane_row = lax.broadcasted_iota(jnp.int32, (48, 128), 0)
    pick = jnp.where((lane_row == 5) | (lane_row == 29) | (lane_row == 45), 1.0, 0.0).astype(jnp.bfloat16)

    for copy in first:
        copy.wait()

    def prepare(cell, carry):
        cell_x, cell_y, cell_z = cell // 16, (cell // 4) % 4, cell % 4
        tile = field[cell_x, cell_y, cell_z]
        row, where_at = placed(tile, cell_x, cell_y, cell_z)
        mass = tile[3:4]
        norm = jnp.sum(jnp.where(row < 3, where_at * where_at, 0.0), axis=0, keepdims=True)
        moving = jnp.sum(jnp.where(row < 3, where_at * pltpu.roll(tile, 4, 0), 0.0), axis=0, keepdims=True)
        given = jnp.where(
            row < 3,
            where_at,
            jnp.where(row == 3, norm, jnp.where(row == 4, 1.0, jnp.where(row == 5, mass, 0.0))),
        )
        high, middle, low = thirds(given)
        stack = jnp.concatenate([high, high, high, middle, middle, low], axis=0)
        turned = jnp.transpose(stack).astype(jnp.bfloat16)
        feat[cell] = turned
        mass_b[cell] = jnp.dot(turned, pick, preferred_element_type=f32)
        column = jnp.where(row == 3, 1.0, jnp.where(row == 7, moving, where_at)) * mass
        high, middle, low = thirds(column)
        upper = jnp.concatenate([high, middle, low, jnp.zeros_like(low)], axis=0).astype(jnp.bfloat16)
        lower = jnp.concatenate([high, middle, jnp.zeros_like(low), jnp.zeros_like(low)], axis=0).astype(jnp.bfloat16)
        col_a[cell] = jnp.concatenate([upper, lower], axis=1)
        return carry

    lax.fori_loop(0, 64, prepare, 0)

    def density_of(total, length):
        cube = length * length * length
        return (2.0 * KERNEL_NORM) * jnp.sum(total, axis=0, keepdims=True) / (cube * cube)

    def parts_of(target):
        return target // 4, (target // 2) % 2, target % 2

    def base_of(target):
        tx, ty, tz = parts_of(target)
        return tx * 16 + ty * 4 + tz

    def weigh(radius, three_square, length, half, half_cube):
        gap = jnp.maximum(length - radius, 0.0)
        return jnp.where(radius < half, half_cube - three_square * gap, gap * gap * gap)

    def target_fields(target):
        tx, ty, tz = parts_of(target)
        tile = field[1 + tx, 1 + ty, 1 + tz]
        row, where_at = placed(tile, 1 + tx, 1 + ty, 1 + tz)
        return tile, row, where_at

    def first_pass(target, carry):
        tx, ty, tz = parts_of(target)
        tile, row, where_at = target_fields(target)
        norm = jnp.sum(jnp.where(row < 3, where_at * where_at, 0.0), axis=0, keepdims=True)
        given = jnp.where(row < 3, -2.0 * where_at, jnp.where(row == 3, 1.0, jnp.where(row == 4, norm, 0.0)))
        high, middle, low = thirds(given)
        target_feat = jnp.concatenate([high, middle, low, high, middle, high], axis=0).astype(jnp.bfloat16)
        length = smooth_ref[tx, ty, pl.ds(tz, 1)]
        half = 0.5 * length
        half_cube = half * length * length
        base = base_of(target)
        total = jnp.zeros((8, 128), f32)
        for place, offset in enumerate(OFFSETS):
            flat = jnp.maximum(jnp.dot(feat[base + offset], target_feat, preferred_element_type=f32), TINY)
            radius = flat * lax.rsqrt(flat)
            three_square = 3.0 * flat
            dist[target, place] = radius
            square[target, place] = three_square
            total = total + fold(mass_b[base + offset] * weigh(radius, three_square, length, half, half_cube))
        density = density_of(total, length)
        tfeat[target, 0:1] = ETA * cube_root(tile[3:4] / density)
        return carry

    lax.fori_loop(0, 8, first_pass, 0)

    def second_pass(target, carry):
        tx, ty, tz = parts_of(target)
        tile = field[1 + tx, 1 + ty, 1 + tz]
        mass, energy = tile[3:4], tile[7:8]
        length = tfeat[target, 0:1]
        half = 0.5 * length
        half_cube = half * length * length
        base = base_of(target)
        total = jnp.zeros((8, 128), f32)
        for place, offset in enumerate(OFFSETS):
            total = total + fold(
                mass_b[base + offset] * weigh(dist[target, place], square[target, place], length, half, half_cube)
            )
        density = density_of(total, length)
        length = ETA * cube_root(mass / density)
        dens_ref[tx, ty, pl.ds(tz, 1)] = density
        cube = length * length * length
        ratio = (GAMMA - 1.0) * energy / density / (cube * cube)
        tfeat[target, 1:2] = ratio
        late[1 + tx, 1 + ty, 1 + tz, 0:1] = length
        late[1 + tx, 1 + ty, 1 + tz, 1:2] = mass * ratio
        return carry

    lax.fori_loop(0, 8, second_pass, 0)

    second = exchange(late, send_late, recv_late)
    for copy in second:
        copy.start()
    for copy in second:
        copy.wait()

    def prepare_late(cell, carry):
        cell_x, cell_y, cell_z = cell // 16, (cell // 4) % 4, cell % 4
        row, where_at = placed(field[cell_x, cell_y, cell_z], cell_x, cell_y, cell_z)
        values = late[cell_x, cell_y, cell_z]
        len_b[cell] = jnp.transpose(jnp.broadcast_to(values[0:1], (128, 128)))
        column = jnp.where(row == 3, 1.0, jnp.where(row < 3, where_at, 0.0)) * values[1:2]
        high, middle, low = thirds(column)
        upper = jnp.concatenate([high, middle, low, jnp.zeros_like(low)], axis=0).astype(jnp.bfloat16)
        lower = jnp.concatenate([high, middle, jnp.zeros_like(low), jnp.zeros_like(low)], axis=0).astype(jnp.bfloat16)
        col_b[cell] = jnp.concatenate([upper, lower], axis=1)
        return carry

    lax.fori_loop(0, 64, prepare_late, 0)

    def halves(value):
        high = value.astype(jnp.bfloat16)
        low = (value - high.astype(f32)).astype(jnp.bfloat16)
        return jnp.concatenate([high, low], axis=0)

    def force(target, carry):
        tx, ty, tz = parts_of(target)
        tile, row, where_at = target_fields(target)
        length = late[1 + tx, 1 + ty, 1 + tz, 0:1]
        steep = (2.0 / ROOT3) * length
        base = base_of(target)
        own = jnp.zeros((32, 128), f32)
        theirs = jnp.zeros((32, 128), f32)
        for place, offset in enumerate(OFFSETS):
            radius = dist[target, place]
            inverse = lax.rsqrt(square[target, place])
            twice = radius + radius
            scaled = ROOT3 * radius
            gap = jnp.maximum(length - radius, 0.0)
            slope = jnp.where(twice < length, steep - scaled, gap * gap * inverse)
            own = own + jnp.dot(col_a[base + offset], halves(slope), preferred_element_type=f32)
            their_length = len_b[base + offset]
            gap = jnp.maximum(their_length - radius, 0.0)
            slope = jnp.where(
                twice < their_length, (2.0 / ROOT3) * their_length - scaled, gap * gap * inverse
            )
            theirs = theirs + jnp.dot(col_b[base + offset], halves(slope), preferred_element_type=f32)
        own = own[0:8] + (own[8:16] + own[16:24])
        theirs = theirs[0:8] + (theirs[8:16] + theirs[16:24])
        on = active_ref[tx, ty, pl.ds(tz, 1)].astype(f32)
        scale = (6.0 * ROOT3 * KERNEL_NORM) * on
        ratio = tfeat[target, 1:2]
        push = scale * (ratio * (where_at * own[3:4] - own) + (where_at * theirs[3:4] - theirs))
        for c in range(3):
            acc_ref[c, tx, ty, pl.ds(tz, 1)] = push[c : c + 1]
        speed = pltpu.roll(tile, 4, 0)
        slide = pltpu.roll(own, 4, 0)
        mixed = speed * (where_at * own[3:4] - own) - where_at * slide
        heat = jnp.sum(jnp.where(row < 3, mixed, 0.0), axis=0, keepdims=True) + own[7:8]
        heat_ref[tx, ty, pl.ds(tz, 1)] = -scale * ratio * heat
        return carry

    lax.fori_loop(0, 8, force, 0)


def body(offsets, masses, smoothing, velocity, energy, active):
    f32, bf16 = jnp.float32, jnp.bfloat16
    vmem = pl.BlockSpec(memory_space=pltpu.VMEM)
    count = len(DIRECTIONS)
    return pl.pallas_call(
        kernel,
        out_shape=(
            jax.ShapeDtypeStruct(masses.shape, f32),
            jax.ShapeDtypeStruct(offsets.shape, f32),
            jax.ShapeDtypeStruct(masses.shape, f32),
        ),
        in_specs=[vmem] * 6,
        out_specs=(vmem, vmem, vmem),
        scratch_shapes=[
            pltpu.VMEM((4, 4, 4, 8, 128), f32),
            pltpu.VMEM((4, 4, 4, 2, 128), f32),
            pltpu.VMEM((64, 128, 48), bf16),
            pltpu.VMEM((8, 8, 128), f32),
            pltpu.VMEM((64, 128, 128), f32),
            pltpu.VMEM((64, 128, 128), f32),
            pltpu.VMEM((64, 32, 256), bf16),
            pltpu.VMEM((64, 32, 256), bf16),
            pltpu.VMEM((8, 27, 128, 128), f32),
            pltpu.VMEM((8, 27, 128, 128), f32),
            pltpu.SemaphoreType.DMA((count,)),
            pltpu.SemaphoreType.DMA((count,)),
            pltpu.SemaphoreType.DMA((count,)),
            pltpu.SemaphoreType.DMA((count,)),
        ],
        compiler_params=pltpu.CompilerParams(collective_id=0, has_side_effects=True, vmem_limit_bytes=60 * 1024 * 1024),
    )(offsets, masses, smoothing, velocity, energy, active)


def solution(mesh):
    in_specs = (
        P(None, "gx", "gy", "gz", None),
        P("gx", "gy", "gz", None),
        P("gx", "gy", "gz", None),
        P(None, "gx", "gy", "gz", None),
        P("gx", "gy", "gz", None),
        P("gx", "gy", "gz", None),
    )
    out_specs = (
        P("gx", "gy", "gz", None),
        P(None, "gx", "gy", "gz", None),
        P("gx", "gy", "gz", None),
    )
    return jax.shard_map(body, mesh=mesh, in_specs=in_specs, out_specs=out_specs, check_vma=False)
```

profile of v0, /device:TPU:1, one launch (start us, length us, event | category | flops | bytes accessed | tf_op | source)
XLA Modules:
  0.0 88.1 jit_solution(5637991888777856460)
XLA Ops:
  0.6 85.0 %shard_map.85 = (f32[2,2,2,128]{3,2,1,0:T(2,128)}, f32[3,2,2,2,128]{4,3,2,1,0:T(2,128)}, f32[2,2,2,128]{3,2,1,0:T(2,128)}) custom-call(f32[3,2,2,2,128]{4,3,2,1,0:T(2,128)} %off_ref.1, f32[2,2,2,128]{3,2,1,0:T(2,128)} %mass_ref.1, f32[2,2,2,128]{3,2,1,0:T(2,128)} %smooth_ref.1, f32[3,2,2,2,128]{4,3,2,1,0:T(2,128)} %vel_ref.1, f32[2,2,2,128]{3,2,1,0:T(2,128)} %energy_ref.1, ...), custom_call_target="tpu_custom_call" | custom-call | tf_op jit(solution)/shard_map/pallas_call | solution.py:306
  85.6 0.0 copy-start
  85.6 1.3 %copy.12 = f32[2,2,2,128]{3,2,1,0:T(2,128)} copy(f32[2,2,2,128]{3,2,1,0:T(2,128)} %get-tuple-element.6) | data formatting | bytes 8192
  86.9 0.0 copy-done
  86.9 0.0 copy-start.1
  86.9 0.6 copy.13
  87.5 0.1 copy-done.1
  87.6 0.6 copy.14
Async XLA Ops:
  85.6 1.3 %copy-start = (f32[3,2,2,2,128]{4,3,2,1,0:T(2,128)S(1)}, f32[3,2,2,2,128]{4,3,2,1,0:T(2,128)}, u32[]{:S(2)}) copy-start(f32[3,2,2,2,128]{4,3,2,1,0:T(2,128)} %get-tuple-element.7) | copy-start | bytes 36868
  86.9 0.7 copy-start.1
where the time goes:
time: 88.4 us; the launch traced here: 88.1 us
  Pallas kernels  85 us (96%)
  local copies, waits for them, and re-layouts  2.55 us (3%)
    pallas_call x1, Pallas kernels, body(): pl.pallas_call(kernel, out_shape=(jax.ShapeDtypeStruct(masses.shape, f32)...  85 us
    unnamed x7, local copies, waits for them, and re-layouts  2.55 us

commit v1 on v0

v1 whole, which is shorter than its diff:
```python
import functools

import jax
import jax.numpy as jnp
from jax import lax
from jax.experimental import pallas as pl
from jax.experimental.pallas import tpu as pltpu
from jax.sharding import PartitionSpec as P

MESH = pl.DeviceIdType.MESH
AXES = ("gx", "gy", "gz")
KERNEL_NORM = 2.5464790894703255
ETA = 2.3
GAMMA = 5.0 / 3.0
ROOT3 = 3.0**0.5
TINY = 1e-12
DIRECTIONS = [
    (dx, dy, dz) for dx in (-1, 0, 1) for dy in (-1, 0, 1) for dz in (-1, 0, 1) if (dx, dy, dz) != (0, 0, 0)
]
STEPS = [(a, b, c) for a in range(3) for b in range(3) for c in range(3)]


def source_part(step):
    return slice(2, 3) if step == 1 else slice(1, 2) if step == -1 else slice(1, 3)


def landing_part(step):
    return slice(0, 1) if step == 1 else slice(3, 4) if step == -1 else slice(1, 3)


def neighbour(direction):
    found = {}
    for axis, step in zip(AXES, direction):
        count = lax.axis_size(axis)
        found[axis] = lax.rem(lax.axis_index(axis) + count + step, count)
    return tuple(found[axis] for axis in AXES)


def inbox_part(step):
    return slice(0, 1) if step == 1 else slice(1, 2) if step == -1 else slice(0, 2)


def exchange(buffer, inbox, send_sem, recv_sem):
    copies = []
    for place, direction in enumerate(DIRECTIONS):
        if inbox is None:
            source = buffer.at[tuple(source_part(step) for step in direction)]
            target = buffer.at[tuple(landing_part(step) for step in direction)]
        else:
            source = buffer.at[tuple(landing_part(-step) for step in direction)]
            target = inbox.at[(place,) + tuple(inbox_part(step) for step in direction)]
        copies.append(
            pltpu.make_async_remote_copy(
                src_ref=source,
                dst_ref=target,
                send_sem=send_sem.at[place],
                recv_sem=recv_sem.at[place],
                device_id=neighbour(direction),
                device_id_type=MESH,
            )
        )
    return copies


def rounded(value):
    return value.astype(jnp.bfloat16).astype(jnp.float32)


def thirds(value):
    high = rounded(value)
    rest = value - high
    middle = rounded(rest)
    return high, middle, rest - middle


def cube_root(value):
    guess = jnp.exp(jnp.log(value) * (1.0 / 3.0))
    return (2.0 * guess + value / (guess * guess)) * (1.0 / 3.0)


def fold(tile):
    parts = [tile[8 * i : 8 * i + 8] for i in range(tile.shape[0] // 8)]
    while len(parts) > 1:
        parts = [parts[i] + parts[i + 1] for i in range(0, len(parts) - 1, 2)] + (
            [parts[-1]] if len(parts) % 2 else []
        )
    return parts[0]


def placed(tile, cell_x, cell_y, cell_z):
    row = lax.broadcasted_iota(jnp.int32, (8, 128), 0)
    shift = jnp.where(
        row == 0,
        jnp.float32(cell_x) - 2.0,
        jnp.where(row == 1, jnp.float32(cell_y) - 2.0, jnp.where(row == 2, jnp.float32(cell_z) - 2.0, 0.0)),
    )
    return row, tile + shift


def kernel(
    off_ref,
    mass_ref,
    smooth_ref,
    vel_ref,
    energy_ref,
    active_ref,
    dens_ref,
    acc_ref,
    heat_ref,
    field,
    outbox,
    inbox,
    feat,
    tfeat,
    state,
    mass_b,
    col_a,
    col_b,
    dist,
    square,
    total_ref,
    own_ref,
    react,
    send_sem,
    recv_sem,
    send_late,
    recv_late,
):
    f32 = jnp.float32
    barrier = pltpu.get_barrier_semaphore()
    for direction in DIRECTIONS:
        pl.semaphore_signal(barrier, inc=1, device_id=neighbour(direction), device_id_type=MESH)
    for x in range(2):
        for y in range(2):
            for z in range(2):
                for c in range(3):
                    field[1 + x, 1 + y, 1 + z, c : c + 1] = off_ref[c, x, y, z : z + 1]
                    field[1 + x, 1 + y, 1 + z, 4 + c : 5 + c] = vel_ref[c, x, y, z : z + 1]
                field[1 + x, 1 + y, 1 + z, 3:4] = mass_ref[x, y, z : z + 1]
                field[1 + x, 1 + y, 1 + z, 7:8] = energy_ref[x, y, z : z + 1]
    pl.semaphore_wait(barrier, len(DIRECTIONS))
    first = exchange(field, None, send_sem, recv_sem)
    for copy in first:
        copy.start()

    lane_row = lax.broadcasted_iota(jnp.int32, (48, 128), 0)
    pick = jnp.where((lane_row == 5) | (lane_row == 29) | (lane_row == 45), 1.0, 0.0).astype(jnp.bfloat16)

    def parts_of(target):
        return target // 4, (target // 2) % 2, target % 2

    def prepare(cell_x, cell_y, cell_z):
        cell = cell_x * 16 + cell_y * 4 + cell_z
        tile = field[cell_x, cell_y, cell_z]
        row, where_at = placed(tile, cell_x, cell_y, cell_z)
        mass = tile[3:4]
        norm = jnp.sum(jnp.where(row < 3, where_at * where_at, 0.0), axis=0, keepdims=True)
        moving = jnp.sum(jnp.where(row < 3, where_at * pltpu.roll(tile, 4, 0), 0.0), axis=0, keepdims=True)
        given = jnp.where(
            row < 3,
            where_at,
            jnp.where(row == 3, norm, jnp.where(row == 4, 1.0, jnp.where(row == 5, mass, 0.0))),
        )
        high, middle, low = thirds(given)
        stack = jnp.concatenate([high, high, high, middle, middle, low], axis=0)
        turned = jnp.transpose(stack).astype(jnp.bfloat16)
        feat[cell] = turned
        mass_b[cell] = jnp.dot(turned, pick, preferred_element_type=f32)
        column = jnp.where(row == 3, 1.0, jnp.where(row == 7, moving, where_at)) * mass
        high, middle, low = thirds(column)
        zero = jnp.zeros_like(low)
        upper = jnp.concatenate([high, middle, low, zero], axis=0).astype(jnp.bfloat16)
        lower = jnp.concatenate([high, middle, zero, zero], axis=0).astype(jnp.bfloat16)
        col_a[cell] = jnp.concatenate([upper, lower], axis=1)

    def prepare_own(target, carry):
        tx, ty, tz = parts_of(target)
        prepare(1 + tx, 1 + ty, 1 + tz)
        tile = field[1 + tx, 1 + ty, 1 + tz]
        row, where_at = placed(tile, 1 + tx, 1 + ty, 1 + tz)
        norm = jnp.sum(jnp.where(row < 3, where_at * where_at, 0.0), axis=0, keepdims=True)
        given = jnp.where(row < 3, -2.0 * where_at, jnp.where(row == 3, 1.0, jnp.where(row == 4, norm, 0.0)))
        high, middle, low = thirds(given)
        single = jnp.concatenate([high, middle, low, high, middle, high], axis=0)
        high, middle, low = thirds(3.0 * given)
        triple = jnp.concatenate([high, middle, low, high, middle, high], axis=0)
        tfeat[target] = jnp.concatenate([single, triple], axis=1).astype(jnp.bfloat16)
        return carry

    lax.fori_loop(0, 8, prepare_own, 0, unroll=2)

    def weigh(radius, three_square, length, half, half_cube):
        gap = jnp.maximum(length - radius, 0.0)
        return jnp.where(radius < half, half_cube - three_square * gap, gap * gap * gap)

    def remote_steps(target):
        tx, ty, tz = parts_of(target)
        steps = [(2 * tx, b, c) for b in range(3) for c in range(3)]
        steps += [(1 - tx + a, 2 * ty, c) for a in range(2) for c in range(3)]
        steps += [(1 - tx + a, 1 - ty + b, 2 * tz) for a in range(2) for b in range(2)]
        return steps

    def own_steps(target):
        tx, ty, tz = parts_of(target)
        return [(1 - tx + a, 1 - ty + b, 1 - tz + c) for a in range(2) for b in range(2) for c in range(2)]

    def cell_of(target, step):
        tx, ty, tz = parts_of(target)
        return (tx + step[0]) * 16 + (ty + step[1]) * 4 + (tz + step[2])

    def place_of(step):
        return step[0] * 9 + step[1] * 3 + step[2]

    def first_sum(target, steps):
        tx, ty, tz = parts_of(target)
        length = smooth_ref[tx, ty, pl.ds(tz, 1)]
        half = 0.5 * length
        half_cube = half * length * length
        target_feat = tfeat[target]
        total = jnp.zeros((8, 128), f32)
        for step in steps:
            cell, place = cell_of(target, step), place_of(step)
            both = jnp.dot(feat[cell], target_feat, preferred_element_type=f32)
            flat = jnp.maximum(both[:, :128], TINY)
            three_square = both[:, 128:]
            radius = flat * lax.rsqrt(flat)
            dist[target, place] = radius
            square[target, place] = three_square
            total = total + fold(mass_b[cell] * weigh(radius, three_square, length, half, half_cube))
        return length, total

    def first_own(target, carry):
        total_ref[target] = first_sum(target, own_steps(target))[1]
        return carry

    lax.fori_loop(0, 8, first_own, 0)

    for copy in first:
        copy.wait()

    for part, (low_x, high_x, low_y, high_y, low_z, high_z, step_x, step_y, step_z) in enumerate(
        [(0, 4, 0, 4, 0, 4, 3, 1, 1), (1, 3, 0, 4, 0, 4, 1, 3, 1), (1, 3, 1, 3, 0, 4, 1, 1, 3)]
    ):
        cells = [
            (x, y, z)
            for x in range(low_x, high_x, step_x)
            for y in range(low_y, high_y, step_y)
            for z in range(low_z, high_z, step_z)
        ]
        count_y, count_z = len(range(low_y, high_y, step_y)), len(range(low_z, high_z, step_z))

        def prepare_remote(index, carry):
            prepare(
                low_x + step_x * (index // (count_y * count_z)),
                low_y + step_y * (index // count_z % count_y),
                low_z + step_z * (index % count_z),
            )
            return carry

        lax.fori_loop(0, len(cells), prepare_remote, 0, unroll=4)

    def density_of(total, length):
        cube = length * length * length
        return (2.0 * KERNEL_NORM) * jnp.sum(total, axis=0, keepdims=True) / (cube * cube)

    def target_fields(target):
        tx, ty, tz = parts_of(target)
        tile = field[1 + tx, 1 + ty, 1 + tz]
        row, where_at = placed(tile, 1 + tx, 1 + ty, 1 + tz)
        return tile, row, where_at

    def first_rest(target, carry):
        length, total = first_sum(target, remote_steps(target))
        tile, row, where_at = target_fields(target)
        density = density_of(total_ref[target] + total, length)
        state[target, 0:1] = ETA * cube_root(tile[3:4] / density)
        return carry

    lax.fori_loop(0, 8, first_rest, 0)

    def second_pass(target, carry):
        tx, ty, tz = parts_of(target)
        length = state[target, 0:1]
        half = 0.5 * length
        half_cube = half * length * length

        def rows(index, total):
            for c in range(3):
                cell = (tx + index // 3) * 16 + (ty + index % 3) * 4 + tz + c
                place = index * 3 + c
                total = total + fold(
                    mass_b[cell] * weigh(dist[target, place], square[target, place], length, half, half_cube)
                )
            return total

        total = lax.fori_loop(0, 9, rows, jnp.zeros((8, 128), f32))
        tile, row, where_at = target_fields(target)
        mass, energy = tile[3:4], tile[7:8]
        density = density_of(total, length)
        length = ETA * cube_root(mass / density)
        dens_ref[tx, ty, pl.ds(tz, 1)] = density
        cube = length * length * length
        ratio = (GAMMA - 1.0) * energy / density / (cube * cube)
        state[target, 0:1] = length
        state[target, 1:2] = ratio
        column = jnp.where(row == 3, 1.0, jnp.where(row < 3, where_at, 0.0)) * (mass * ratio)
        high, middle, low = thirds(column)
        pair = jnp.where(row < 4, high, pltpu.roll(middle, 4, 0))
        upper = jnp.concatenate([pair, low], axis=0).astype(jnp.bfloat16)
        lower = jnp.concatenate([pair, jnp.zeros_like(low)], axis=0).astype(jnp.bfloat16)
        col_b[target] = jnp.concatenate([upper, lower], axis=1)
        return carry

    lax.fori_loop(0, 8, second_pass, 0)

    def clear(index, carry):
        react[index] = jnp.zeros((16, 128), f32)
        return carry

    lax.fori_loop(0, 64, clear, 0, unroll=8)

    def force(target, steps):
        length = state[target, 0:1]
        half = 0.5 * length
        steep = (2.0 / ROOT3) * length
        beta = col_b[target]
        own = jnp.zeros((32, 128), f32)
        for step in steps:
            cell, place = cell_of(target, step), place_of(step)
            radius = dist[target, place]
            inverse = lax.rsqrt(square[target, place])
            gap = jnp.maximum(length - radius, 0.0)
            slope = jnp.where(radius < half, steep - ROOT3 * radius, gap * gap * inverse)
            high = slope.astype(jnp.bfloat16)
            low = (slope - high.astype(f32)).astype(jnp.bfloat16)
            own = own + jnp.dot(col_a[cell], jnp.concatenate([high, low], axis=0), preferred_element_type=f32)
            react[cell] += lax.dot_general(
                beta,
                jnp.concatenate([high, low], axis=1),
                (((1,), (1,)), ((), ())),
                preferred_element_type=f32,
            )
        return own

    def settled(cell, tile, cell_x, cell_y, cell_z):
        row, where_at = placed(tile, cell_x, cell_y, cell_z)
        parts = react[cell]
        parts = parts[0:8] + (pltpu.roll(parts[0:8], 4, 0) + parts[8:16])
        return where_at * parts[3:4] - parts

    def force_remote(target, carry):
        own_ref[target] = force(target, remote_steps(target))
        return carry

    lax.fori_loop(0, 8, force_remote, 0)

    def post(cell, carry):
        cell_x, cell_y, cell_z = cell // 16, cell // 4 % 4, cell % 4
        outbox[cell_x, cell_y, cell_z] = settled(cell, field[cell_x, cell_y, cell_z], cell_x, cell_y, cell_z)[0:4]
        return carry

    lax.fori_loop(0, 64, post, 0, unroll=4)
    second = exchange(outbox, inbox, send_late, recv_late)
    for copy in second:
        copy.start()

    def force_own(target, carry):
        own_ref[target] += force(target, own_steps(target))
        return carry

    lax.fori_loop(0, 8, force_own, 0)

    for copy in second:
        copy.wait()

    for target in range(8):
        tx, ty, tz = target // 4, target // 2 % 2, target % 2
        tile = field[1 + tx, 1 + ty, 1 + tz]
        cell = (1 + tx) * 16 + (1 + ty) * 4 + 1 + tz
        row, where_at = placed(tile, 1 + tx, 1 + ty, 1 + tz)
        theirs = settled(cell, tile, 1 + tx, 1 + ty, 1 + tz)[0:4]
        for place, direction in enumerate(DIRECTIONS):
            spans = [inbox_part(step) for step in direction]
            if all(span.start <= at < span.stop for span, at in zip(spans, (tx, ty, tz))):
                theirs = theirs + inbox[place, tx, ty, tz]
        own = own_ref[target]
        own = own[0:8] + (own[8:16] + own[16:24])
        on = active_ref[tx, ty, tz : tz + 1].astype(f32)
        scale = (6.0 * ROOT3 * KERNEL_NORM) * on
        ratio = state[target, 1:2]
        bare = where_at * own[3:4] - own
        push = scale * (ratio * bare[0:3] + theirs[0:3])
        for c in range(3):
            acc_ref[c, tx, ty, tz : tz + 1] = push[c : c + 1]
        mixed = pltpu.roll(tile, 4, 0) * bare - where_at * pltpu.roll(own, 4, 0)
        heat = jnp.sum(jnp.where(row < 3, mixed, 0.0), axis=0, keepdims=True) + own[7:8]
        heat_ref[tx, ty, tz : tz + 1] = -scale * ratio * heat


def body(offsets, masses, smoothing, velocity, energy, active):
    f32, bf16 = jnp.float32, jnp.bfloat16
    vmem = pl.BlockSpec(memory_space=pltpu.VMEM)
    count = len(DIRECTIONS)
    return pl.pallas_call(
        kernel,
        out_shape=(
            jax.ShapeDtypeStruct(masses.shape, f32),
            jax.ShapeDtypeStruct(offsets.shape, f32),
            jax.ShapeDtypeStruct(masses.shape, f32),
        ),
        in_specs=[vmem] * 6,
        out_specs=(vmem, vmem, vmem),
        scratch_shapes=[
            pltpu.VMEM((4, 4, 4, 8, 128), f32),
            pltpu.VMEM((4, 4, 4, 4, 128), f32),
            pltpu.VMEM((count, 2, 2, 2, 4, 128), f32),
            pltpu.VMEM((64, 128, 48), bf16),
            pltpu.VMEM((8, 48, 256), bf16),
            pltpu.VMEM((8, 8, 128), f32),
            pltpu.VMEM((64, 128, 128), f32),
            pltpu.VMEM((64, 32, 256), bf16),
            pltpu.VMEM((8, 16, 256), bf16),
            pltpu.VMEM((8, 27, 128, 128), f32),
            pltpu.VMEM((8, 27, 128, 128), f32),
            pltpu.VMEM((8, 8, 128), f32),
            pltpu.VMEM((8, 32, 128), f32),
            pltpu.VMEM((64, 16, 128), f32),
            pltpu.SemaphoreType.DMA((count,)),
            pltpu.SemaphoreType.DMA((count,)),
            pltpu.SemaphoreType.DMA((count,)),
            pltpu.SemaphoreType.DMA((count,)),
        ],
        compiler_params=pltpu.CompilerParams(collective_id=0, has_side_effects=True, vmem_limit_bytes=60 * 1024 * 1024),
    )(offsets, masses, smoothing, velocity, energy, active)


def solution(mesh):
    in_specs = (
        P(None, "gx", "gy", "gz", None),
        P("gx", "gy", "gz", None),
        P("gx", "gy", "gz", None),
        P(None, "gx", "gy", "gz", None),
        P("gx", "gy", "gz", None),
        P("gx", "gy", "gz", None),
    )
    out_specs = (
        P("gx", "gy", "gz", None),
        P(None, "gx", "gy", "gz", None),
        P("gx", "gy", "gz", None),
    )
    return jax.shard_map(body, mesh=mesh, in_specs=in_specs, out_specs=out_specs, check_vma=False)
```

time: 88.4 us -> 60.9 us (0.69)
  Pallas kernels: 85 us -> 57.4 us
    pallas_call x1, Pallas kernels: 85 us -> 57.4 us  [body(): pl.pallas_call(kernel, out_shape=(jax.ShapeDtypeStruct(masses.shape, f32)...]
where the time goes in v1:
time: 60.9 us; the launch traced here: 60.6 us
  Pallas kernels  57.4 us (94%)
  local copies, waits for them, and re-layouts  2.55 us (4%)
  between operations  0.65 us (1%)
    pallas_call x1, Pallas kernels, body(): pl.pallas_call(kernel, out_shape=(jax.ShapeDtypeStruct(masses.shape, f32)...  57.4 us
    unnamed x7, local copies, waits for them, and re-layouts  2.55 us

profile of v1, /device:TPU:1, one launch (start us, length us, event | category | flops | bytes accessed | tf_op | source)
XLA Modules:
  0.0 60.6 jit_solution(13256863701466980420)
XLA Ops:
  0.6 57.4 %shard_map.85 = (f32[2,2,2,128]{3,2,1,0:T(2,128)}, f32[3,2,2,2,128]{4,3,2,1,0:T(2,128)}, f32[2,2,2,128]{3,2,1,0:T(2,128)}) custom-call(f32[3,2,2,2,128]{4,3,2,1,0:T(2,128)} %off_ref.1, f32[2,2,2,128]{3,2,1,0:T(2,128)} %mass_ref.1, f32[2,2,2,128]{3,2,1,0:T(2,128)} %smooth_ref.1, f32[3,2,2,2,128]{4,3,2,1,0:T(2,128)} %vel_ref.1, f32[2,2,2,128]{3,2,1,0:T(2,128)} %energy_ref.1, ...), custom_call_target="tpu_custom_call" | custom-call | tf_op jit(solution)/shard_map/pallas_call | solution.py:404
  58.1 0.0 copy-start
  58.1 1.3 %copy.12 = f32[2,2,2,128]{3,2,1,0:T(2,128)} copy(f32[2,2,2,128]{3,2,1,0:T(2,128)} %get-tuple-element.6) | data formatting | bytes 8192
  59.4 0.0 copy-done
  59.4 0.0 copy-start.1
  59.4 0.6 copy.13
  60.0 0.1 copy-done.1
  60.0 0.6 copy.14
Async XLA Ops:
  58.1 1.3 %copy-start = (f32[3,2,2,2,128]{4,3,2,1,0:T(2,128)S(1)}, f32[3,2,2,2,128]{4,3,2,1,0:T(2,128)}, u32[]{:S(2)}) copy-start(f32[3,2,2,2,128]{4,3,2,1,0:T(2,128)} %get-tuple-element.7) | copy-start | bytes 36868
  59.4 0.7 %copy-start.1 = (f32[2,2,2,128]{3,2,1,0:T(2,128)S(1)}, f32[2,2,2,128]{3,2,1,0:T(2,128)}, u32[]{:S(2)}) copy-start(f32[2,2,2,128]{3,2,1,0:T(2,128)} %get-tuple-element.8) | copy-start | bytes 12292

commit v2 on v1

--- a/solution.py
+++ b/solution.py
@@ -13,7 +13,7 @@
 ETA = 2.3
 GAMMA = 5.0 / 3.0
 ROOT3 = 3.0**0.5
-TINY = 1e-12
+TINY = 1e-7
 DIRECTIONS = [
     (dx, dy, dz) for dx in (-1, 0, 1) for dy in (-1, 0, 1) for dz in (-1, 0, 1) if (dx, dy, dz) != (0, 0, 0)
 ]
@@ -28,19 +28,23 @@
     return slice(0, 1) if step == 1 else slice(3, 4) if step == -1 else slice(1, 3)
 
 
-def neighbour(direction):
-    found = {}
-    for axis, step in zip(AXES, direction):
-        count = lax.axis_size(axis)
-        found[axis] = lax.rem(lax.axis_index(axis) + count + step, count)
-    return tuple(found[axis] for axis in AXES)
+def rings():
+    found = []
+    for axis in AXES:
+        count, me = lax.axis_size(axis), lax.axis_index(axis)
+        found.append((me, lax.rem(me + 1, count), lax.rem(me + count - 1, count)))
+    return found
+
+
+def neighbour(ring, direction):
+    return tuple(places[step] for places, step in zip(ring, direction))
 
 
 def inbox_part(step):
     return slice(0, 1) if step == 1 else slice(1, 2) if step == -1 else slice(0, 2)
 
 
-def exchange(buffer, inbox, send_sem, recv_sem):
+def exchange(ring, buffer, inbox, send_sem, recv_sem):
     copies = []
     for place, direction in enumerate(DIRECTIONS):
         if inbox is None:
@@ -55,7 +59,7 @@
                 dst_ref=target,
                 send_sem=send_sem.at[place],
                 recv_sem=recv_sem.at[place],
-                device_id=neighbour(direction),
+                device_id=neighbour(ring, direction),
                 device_id_type=MESH,
             )
         )
@@ -103,10 +107,7 @@
     smooth_ref,
     vel_ref,
     energy_ref,
-    active_ref,
-    dens_ref,
-    acc_ref,
-    heat_ref,
+    out_ref,
     field,
     outbox,
     inbox,
@@ -127,9 +128,10 @@
     recv_late,
 ):
     f32 = jnp.float32
+    ring = rings()
     barrier = pltpu.get_barrier_semaphore()
     for direction in DIRECTIONS:
-        pl.semaphore_signal(barrier, inc=1, device_id=neighbour(direction), device_id_type=MESH)
+        pl.semaphore_signal(barrier, inc=1, device_id=neighbour(ring, direction), device_id_type=MESH)
     for x in range(2):
         for y in range(2):
             for z in range(2):
@@ -139,7 +141,7 @@
                 field[1 + x, 1 + y, 1 + z, 3:4] = mass_ref[x, y, z : z + 1]
                 field[1 + x, 1 + y, 1 + z, 7:8] = energy_ref[x, y, z : z + 1]
     pl.semaphore_wait(barrier, len(DIRECTIONS))
-    first = exchange(field, None, send_sem, recv_sem)
+    first = exchange(ring, field, None, send_sem, recv_sem)
     for copy in first:
         copy.start()
 
@@ -221,12 +223,14 @@
         for step in steps:
             cell, place = cell_of(target, step), place_of(step)
             both = jnp.dot(feat[cell], target_feat, preferred_element_type=f32)
-            flat = jnp.maximum(both[:, :128], TINY)
-            three_square = both[:, 128:]
-            radius = flat * lax.rsqrt(flat)
-            dist[target, place] = radius
-            square[target, place] = three_square
-            total = total + fold(mass_b[cell] * weigh(radius, three_square, length, half, half_cube))
+            for at in range(0, 128, 64):
+                rows = slice(at, at + 64)
+                flat = both[rows, :128]
+                three_square = both[rows, 128:]
+                radius = flat * lax.rsqrt(jnp.maximum(flat, TINY))
+                dist[target, place, rows] = radius
+                square[target, place, rows] = three_square
+                total = total + fold(mass_b[cell, rows] * weigh(radius, three_square, length, half, half_cube))
         return length, total
 
     def first_own(target, carry):
@@ -238,26 +242,19 @@
     for copy in first:
         copy.wait()
 
-    for part, (low_x, high_x, low_y, high_y, low_z, high_z, step_x, step_y, step_z) in enumerate(
-        [(0, 4, 0, 4, 0, 4, 3, 1, 1), (1, 3, 0, 4, 0, 4, 1, 3, 1), (1, 3, 1, 3, 0, 4, 1, 1, 3)]
-    ):
-        cells = [
-            (x, y, z)
-            for x in range(low_x, high_x, step_x)
-            for y in range(low_y, high_y, step_y)
-            for z in range(low_z, high_z, step_z)
-        ]
-        count_y, count_z = len(range(low_y, high_y, step_y)), len(range(low_z, high_z, step_z))
-
-        def prepare_remote(index, carry):
-            prepare(
-                low_x + step_x * (index // (count_y * count_z)),
-                low_y + step_y * (index // count_z % count_y),
-                low_z + step_z * (index % count_z),
-            )
-            return carry
-
-        lax.fori_loop(0, len(cells), prepare_remote, 0, unroll=4)
+    def prepare_remote(side, carry):
+        for y in range(4):
+            for z in range(4):
+                prepare(3 * side, y, z)
+        for y in (0, 3):
+            for z in range(4):
+                prepare(1 + side, y, z)
+        for y in (1, 2):
+            for z in (0, 3):
+                prepare(1 + side, y, z)
+        return carry
+
+    lax.fori_loop(0, 2, prepare_remote, 0)
 
     def density_of(total, length):
         cube = length * length * length
@@ -285,20 +282,23 @@
         half_cube = half * length * length
 
         def rows(index, total):
-            for c in range(3):
-                cell = (tx + index // 3) * 16 + (ty + index % 3) * 4 + tz + c
-                place = index * 3 + c
-                total = total + fold(
-                    mass_b[cell] * weigh(dist[target, place], square[target, place], length, half, half_cube)
-                )
+            for at in range(9):
+                cell = (tx + index) * 16 + (ty + at // 3) * 4 + tz + at % 3
+                place = index * 9 + at
+                for first_row in range(0, 128, 64):
+                    at_rows = slice(first_row, first_row + 64)
+                    near = weigh(
+                        dist[target, place, at_rows], square[target, place, at_rows], length, half, half_cube
+                    )
+                    total = total + fold(mass_b[cell, at_rows] * near)
             return total
 
-        total = lax.fori_loop(0, 9, rows, jnp.zeros((8, 128), f32))
+        total = lax.fori_loop(0, 3, rows, jnp.zeros((8, 128), f32))
         tile, row, where_at = target_fields(target)
         mass, energy = tile[3:4], tile[7:8]
         density = density_of(total, length)
         length = ETA * cube_root(mass / density)
-        dens_ref[tx, ty, pl.ds(tz, 1)] = density
+        out_ref[0, tx, ty, pl.ds(tz, 1)] = density
         cube = length * length * length
         ratio = (GAMMA - 1.0) * energy / density / (cube * cube)
         state[target, 0:1] = length
@@ -314,10 +314,10 @@
     lax.fori_loop(0, 8, second_pass, 0)
 
     def clear(index, carry):
-        react[index] = jnp.zeros((16, 128), f32)
-        return carry
-
-    lax.fori_loop(0, 64, clear, 0, unroll=8)
+        react[pl.ds(16 * index, 16)] = jnp.zeros((16, 16, 128), f32)
+        return carry
+
+    lax.fori_loop(0, 4, clear, 0)
 
     def force(target, steps):
         length = state[target, 0:1]
@@ -327,12 +327,15 @@
         own = jnp.zeros((32, 128), f32)
         for step in steps:
             cell, place = cell_of(target, step), place_of(step)
-            radius = dist[target, place]
-            inverse = lax.rsqrt(square[target, place])
-            gap = jnp.maximum(length - radius, 0.0)
-            slope = jnp.where(radius < half, steep - ROOT3 * radius, gap * gap * inverse)
-            high = slope.astype(jnp.bfloat16)
-            low = (slope - high.astype(f32)).astype(jnp.bfloat16)
+            highs, lows = [], []
+            for at in range(0, 128, 64):
+                radius = dist[target, place, at : at + 64]
+                inverse = lax.rsqrt(square[target, place, at : at + 64])
+                gap = jnp.maximum(length - radius, 0.0)
+                slope = jnp.where(radius < half, steep - ROOT3 * radius, gap * gap * inverse)
+                highs.append(slope.astype(jnp.bfloat16))
+                lows.append((slope - highs[-1].astype(f32)).astype(jnp.bfloat16))
+            high, low = jnp.concatenate(highs, axis=0), jnp.concatenate(lows, axis=0)
             own = own + jnp.dot(col_a[cell], jnp.concatenate([high, low], axis=0), preferred_element_type=f32)
             react[cell] += lax.dot_general(
                 beta,
@@ -354,13 +357,14 @@
 
     lax.fori_loop(0, 8, force_remote, 0)
 
-    def post(cell, carry):
-        cell_x, cell_y, cell_z = cell // 16, cell // 4 % 4, cell % 4
-        outbox[cell_x, cell_y, cell_z] = settled(cell, field[cell_x, cell_y, cell_z], cell_x, cell_y, cell_z)[0:4]
-        return carry
-
-    lax.fori_loop(0, 64, post, 0, unroll=4)
-    second = exchange(outbox, inbox, send_late, recv_late)
+    def post(cell_x, carry):
+        for y in range(4):
+            for z in range(4):
+                outbox[cell_x, y, z] = settled(cell_x * 16 + y * 4 + z, field[cell_x, y, z], cell_x, y, z)[0:4]
+        return carry
+
+    lax.fori_loop(0, 4, post, 0)
+    second = exchange(ring, outbox, inbox, send_late, recv_late)
     for copy in second:
         copy.start()
 
@@ -385,31 +389,34 @@
                 theirs = theirs + inbox[place, tx, ty, tz]
         own = own_ref[target]
         own = own[0:8] + (own[8:16] + own[16:24])
-        on = active_ref[tx, ty, tz : tz + 1].astype(f32)
-        scale = (6.0 * ROOT3 * KERNEL_NORM) * on
+        scale = 6.0 * ROOT3 * KERNEL_NORM
         ratio = state[target, 1:2]
         bare = where_at * own[3:4] - own
         push = scale * (ratio * bare[0:3] + theirs[0:3])
         for c in range(3):
-            acc_ref[c, tx, ty, tz : tz + 1] = push[c : c + 1]
+            out_ref[1 + c, tx, ty, tz : tz + 1] = push[c : c + 1]
         mixed = pltpu.roll(tile, 4, 0) * bare - where_at * pltpu.roll(own, 4, 0)
         heat = jnp.sum(jnp.where(row < 3, mixed, 0.0), axis=0, keepdims=True) + own[7:8]
-        heat_ref[tx, ty, tz : tz + 1] = -scale * ratio * heat
+        out_ref[4, tx, ty, tz : tz + 1] = -scale * ratio * heat
+
+
+def finish(result_ref, active_ref, dens_ref, acc_ref, heat_ref):
+    on = active_ref[...].astype(jnp.float32)
+    dens_ref[...] = result_ref[0]
+    for c in range(3):
+        acc_ref[c] = result_ref[1 + c] * on
+    heat_ref[...] = result_ref[4] * on
 
 
 def body(offsets, masses, smoothing, velocity, energy, active):
     f32, bf16 = jnp.float32, jnp.bfloat16
     vmem = pl.BlockSpec(memory_space=pltpu.VMEM)
     count = len(DIRECTIONS)
-    return pl.pallas_call(
+    result = pl.pallas_call(
         kernel,
-        out_shape=(
-            jax.ShapeDtypeStruct(masses.shape, f32),
-            jax.ShapeDtypeStruct(offsets.shape, f32),
-            jax.ShapeDtypeStruct(masses.shape, f32),
-        ),
-        in_specs=[vmem] * 6,
-        out_specs=(vmem, vmem, vmem),
+        out_shape=jax.ShapeDtypeStruct((5,) + masses.shape, f32),
+        in_specs=[vmem] * 5,
+        out_specs=vmem,
         scratch_shapes=[
             pltpu.VMEM((4, 4, 4, 8, 128), f32),
             pltpu.VMEM((4, 4, 4, 4, 128), f32),
@@ -431,7 +438,17 @@
             pltpu.SemaphoreType.DMA((count,)),
         ],
         compiler_params=pltpu.CompilerParams(collective_id=0, has_side_effects=True, vmem_limit_bytes=60 * 1024 * 1024),
-    )(offsets, masses, smoothing, velocity, energy, active)
+    )(offsets, masses, smoothing, velocity, energy)
+    return pl.pallas_call(
+        finish,
+        out_shape=(
+            jax.ShapeDtypeStruct(masses.shape, f32),
+            jax.ShapeDtypeStruct(offsets.shape, f32),
+            jax.ShapeDtypeStruct(masses.shape, f32),
+        ),
+        in_specs=[vmem] * 2,
+        out_specs=(vmem, vmem, vmem),
+    )(result, active)
 
 
 def solution(mesh):

time: 60.9 us -> 54.6 us (0.90)
  Pallas kernels: 57.4 us -> 53.7 us
  local copies, waits for them, and re-layouts: 2.55 us -> 0 us
    pallas_call x1 -> x2, Pallas kernels: 57.4 us -> 53.7 us  [the longest x1 52.4 us: body(): pl.pallas_call(kernel, out_shape=jax.ShapeDtypeStruct((5,) + masses.shape...]
    unnamed x7 -> x0, local copies, waits for them, and re-layouts: 2.55 us -> none
where the time goes in v2:
time: 54.6 us; the launch traced here: 54.4 us
  Pallas kernels  53.7 us (98%)
  between operations  0.64 us (1%)
    pallas_call x1, Pallas kernels, body(): pl.pallas_call(kernel, out_shape=jax.ShapeDtypeStruct((5,) + masses.shape...  52.4 us
    pallas_call x1, Pallas kernels, body(): pl.pallas_call(finish, out_shape=(jax.ShapeDtypeStruct(masses.shape, f32)...  1.34 us

profile of v2, /device:TPU:1, one launch (start us, length us, event | category | flops | bytes accessed | tf_op | source)
XLA Modules:
  0.0 54.4 jit_solution(3987240958302112225)
XLA Ops:
  0.6 52.4 %shard_map.85.result_ref = f32[5,2,2,2,128]{4,3,2,1,0:T(2,128)} custom-call(f32[3,2,2,2,128]{4,3,2,1,0:T(2,128)} %off_ref.1, f32[2,2,2,128]{3,2,1,0:T(2,128)} %mass_ref.1, f32[2,2,2,128]{3,2,1,0:T(2,128)} %smooth_ref.1, f32[3,2,2,2,128]{4,3,2,1,0:T(2,128)} %vel_ref.1, f32[2,2,2,128]{3,2,1,0:T(2,128)} %energy_ref.1), custom_call_target="tpu_custom_call" | custom-call | tf_op jit(solution)/shard_map/pallas_call | solution.py:415
  53.0 1.3 %shard_map.86 = (f32[2,2,2,128]{3,2,1,0:T(2,128)}, f32[3,2,2,2,128]{4,3,2,1,0:T(2,128)}, f32[2,2,2,128]{3,2,1,0:T(2,128)}) custom-call(f32[5,2,2,2,128]{4,3,2,1,0:T(2,128)} %shard_map.85.result_ref, s32[2,2,2,128]{3,2,1,0:T(2,128)} %active_ref.1), custom_call_target="tpu_custom_call" | custom-call | tf_op jit(solution)/shard_map/pallas_call | solution.py:442

commit v3 on v2

--- a/solution.py
+++ b/solution.py
@@ -189,7 +189,7 @@
         tfeat[target] = jnp.concatenate([single, triple], axis=1).astype(jnp.bfloat16)
         return carry
 
-    lax.fori_loop(0, 8, prepare_own, 0, unroll=2)
+    lax.fori_loop(0, 8, prepare_own, 0, unroll=4)
 
     def weigh(radius, three_square, length, half, half_cube):
         gap = jnp.maximum(length - radius, 0.0)
@@ -223,21 +223,18 @@
         for step in steps:
             cell, place = cell_of(target, step), place_of(step)
             both = jnp.dot(feat[cell], target_feat, preferred_element_type=f32)
-            for at in range(0, 128, 64):
-                rows = slice(at, at + 64)
-                flat = both[rows, :128]
-                three_square = both[rows, 128:]
-                radius = flat * lax.rsqrt(jnp.maximum(flat, TINY))
-                dist[target, place, rows] = radius
-                square[target, place, rows] = three_square
-                total = total + fold(mass_b[cell, rows] * weigh(radius, three_square, length, half, half_cube))
+            flat, three_square = both[:, :128], both[:, 128:]
+            radius = flat * lax.rsqrt(jnp.maximum(flat, TINY))
+            dist[target, place] = radius
+            square[target, place] = three_square
+            total = total + fold(mass_b[cell] * weigh(radius, three_square, length, half, half_cube))
         return length, total
 
     def first_own(target, carry):
         total_ref[target] = first_sum(target, own_steps(target))[1]
         return carry
 
-    lax.fori_loop(0, 8, first_own, 0)
+    lax.fori_loop(0, 8, first_own, 0, unroll=4)
 
     for copy in first:
         copy.wait()
@@ -273,7 +270,7 @@
         state[target, 0:1] = ETA * cube_root(tile[3:4] / density)
         return carry
 
-    lax.fori_loop(0, 8, first_rest, 0)
+    lax.fori_loop(0, 8, first_rest, 0, unroll=2)
 
     def second_pass(target, carry):
         tx, ty, tz = parts_of(target)
@@ -285,12 +282,8 @@
             for at in range(9):
                 cell = (tx + index) * 16 + (ty + at // 3) * 4 + tz + at % 3
                 place = index * 9 + at
-                for first_row in range(0, 128, 64):
-                    at_rows = slice(first_row, first_row + 64)
-                    near = weigh(
-                        dist[target, place, at_rows], square[target, place, at_rows], length, half, half_cube
-                    )
-                    total = total + fold(mass_b[cell, at_rows] * near)
+                near = weigh(dist[target, place], square[target, place], length, half, half_cube)
+                total = total + fold(mass_b[cell] * near)
             return total
 
         total = lax.fori_loop(0, 3, rows, jnp.zeros((8, 128), f32))
@@ -327,15 +320,12 @@
         own = jnp.zeros((32, 128), f32)
         for step in steps:
             cell, place = cell_of(target, step), place_of(step)
-            highs, lows = [], []
-            for at in range(0, 128, 64):
-                radius = dist[target, place, at : at + 64]
-                inverse = lax.rsqrt(square[target, place, at : at + 64])
-                gap = jnp.maximum(length - radius, 0.0)
-                slope = jnp.where(radius < half, steep - ROOT3 * radius, gap * gap * inverse)
-                highs.append(slope.astype(jnp.bfloat16))
-                lows.append((slope - highs[-1].astype(f32)).astype(jnp.bfloat16))
-            high, low = jnp.concatenate(highs, axis=0), jnp.concatenate(lows, axis=0)
+            radius = dist[target, place]
+            inverse = lax.rsqrt(square[target, place])
+            gap = jnp.maximum(length - radius, 0.0)
+            slope = jnp.where(radius < half, steep - ROOT3 * radius, gap * gap * inverse)
+            high = slope.astype(jnp.bfloat16)
+            low = (slope - high.astype(f32)).astype(jnp.bfloat16)
             own = own + jnp.dot(col_a[cell], jnp.concatenate([high, low], axis=0), preferred_element_type=f32)
             react[cell] += lax.dot_general(
                 beta,
@@ -355,7 +345,7 @@
         own_ref[target] = force(target, remote_steps(target))
         return carry
 
-    lax.fori_loop(0, 8, force_remote, 0)
+    lax.fori_loop(0, 8, force_remote, 0, unroll=2)
 
     def post(cell_x, carry):
         for y in range(4):
@@ -372,7 +362,7 @@
         own_ref[target] += force(target, own_steps(target))
         return carry
 
-    lax.fori_loop(0, 8, force_own, 0)
+    lax.fori_loop(0, 8, force_own, 0, unroll=4)
 
     for copy in second:
         copy.wait()

time: 54.6 us -> 53.7 us (0.984)
  Pallas kernels: 53.7 us -> 52.8 us
    pallas_call x1, Pallas kernels: 52.4 us -> 51.5 us  [body(): pl.pallas_call(kernel, out_shape=jax.ShapeDtypeStruct((5,) + masses.shape...]
where the time goes in v3:
time: 53.7 us; the launch traced here: 53.5 us
  Pallas kernels  52.8 us (98%)
  between operations  0.64 us (1%)
    pallas_call x1, Pallas kernels, body(): pl.pallas_call(kernel, out_shape=jax.ShapeDtypeStruct((5,) + masses.shape...  51.5 us
    pallas_call x1, Pallas kernels, body(): pl.pallas_call(finish, out_shape=(jax.ShapeDtypeStruct(masses.shape, f32)...  1.34 us

profile of v3, /device:TPU:1, one launch (start us, length us, event | category | flops | bytes accessed | tf_op | source)
XLA Modules:
  0.0 53.5 jit_solution(3770548767248936437)
XLA Ops:
  0.6 51.5 %shard_map.85.result_ref = f32[5,2,2,2,128]{4,3,2,1,0:T(2,128)} custom-call(f32[3,2,2,2,128]{4,3,2,1,0:T(2,128)} %off_ref.1, f32[2,2,2,128]{3,2,1,0:T(2,128)} %mass_ref.1, f32[2,2,2,128]{3,2,1,0:T(2,128)} %smooth_ref.1, f32[3,2,2,2,128]{4,3,2,1,0:T(2,128)} %vel_ref.1, f32[2,2,2,128]{3,2,1,0:T(2,128)} %energy_ref.1), custom_call_target="tpu_custom_call" | custom-call | tf_op jit(solution)/shard_map/pallas_call | solution.py:405
  52.1 1.3 %shard_map.86 = (f32[2,2,2,128]{3,2,1,0:T(2,128)}, f32[3,2,2,2,128]{4,3,2,1,0:T(2,128)}, f32[2,2,2,128]{3,2,1,0:T(2,128)}) custom-call(f32[5,2,2,2,128]{4,3,2,1,0:T(2,128)} %shard_map.85.result_ref, s32[2,2,2,128]{3,2,1,0:T(2,128)} %active_ref.1), custom_call_target="tpu_custom_call" | custom-call | tf_op jit(solution)/shard_map/pallas_call | solution.py:432
